TPU v7x, 32 devices: a whole 2x2x4 slice. The times are simulated.
32 devices in a mesh: dp: 8 (over z, y), ctx: 4 (over x, core).
Axes of the slice: x: 2, y: 2, z: 4, core: 2. Of those that a mesh axis runs over, the one named last changes fastest.
Arguments:
- projected: bfloat16 [8, 512, 3, 4096], P('dp', 'ctx'), may hold values from -6 to 6
- short_taps: float32 [3, 3, 4096], P(None, None, 'ctx'), may hold values from -3 to 3
- long_filter: bfloat16 [512, 4096], P('dp', 'ctx'), may hold values from -1.1 to 1.1
- skip_gain: float32 [4096], P('ctx'), may hold values from -4 to 4
Outputs:
- mixed: bfloat16 [8, 512, 4096], P('dp', 'ctx')
All inputs are finite; a program needn't handle non-finite values.
Results may differ from a plain program's by a relative error of at most 0.012.
Values may be sent and summed in bfloat16 or wider, within the bound.
A program may use at most 64 MiB of HBM per device.

v0:
```python
import math
import jax
import jax.numpy as jnp
from jax import lax
from jax.sharding import PartitionSpec as P

RADIX = 64
HIGH = lax.Precision.HIGHEST


def causal_short(extended, taps, kernel_size):
    row_count = extended.shape[0] - (kernel_size - 1)
    widened = extended.astype(jnp.float32)
    summed = jnp.zeros((row_count,) + widened.shape[1:], jnp.float32)
    for tap_index in range(kernel_size):
        offset = kernel_size - 1 - tap_index
        summed = summed + taps[tap_index] * widened[offset : offset + row_count]
    return (summed[:, 0].astype(jnp.bfloat16), (summed[:, 1] * summed[:, 2]).astype(jnp.bfloat16))


def dft_tables(length, radix_size):
    outer_size = 2 * length // radix_size
    total_size = outer_size * radix_size
    outer_range = jnp.arange(outer_size, dtype=jnp.int32)
    inner_range = jnp.arange(radix_size, dtype=jnp.int32)
    angle_one = (
        2.0
        * math.pi
        / outer_size
        * (outer_range[:, None] * outer_range[None, :] % outer_size).astype(jnp.float32)
    )
    angle_twist = (
        2.0
        * math.pi
        / total_size
        * (outer_range[:, None] * inner_range[None, :] % total_size).astype(jnp.float32)
    )
    angle_two = (
        2.0
        * math.pi
        / radix_size
        * (inner_range[:, None] * inner_range[None, :] % radix_size).astype(jnp.float32)
    )
    twist_cos = jnp.cos(angle_twist)[:, :, None]
    twist_sin = jnp.sin(angle_twist)[:, :, None]
    return (
        jnp.cos(angle_one),
        jnp.sin(angle_one),
        twist_cos,
        twist_sin,
        jnp.cos(angle_two),
        jnp.sin(angle_two),
    )


def forward_dft(signal, tables, radix_size):
    cos_one, sin_one, twist_cos, twist_sin, cos_two, sin_two = tables
    outer_size = cos_one.shape[0]
    half_size = outer_size // 2
    block_width = signal.shape[1]
    shaped = signal.reshape(half_size, radix_size * block_width)
    first_re = jnp.dot(cos_one[:, :half_size], shaped, precision=HIGH).reshape(
        outer_size, radix_size, block_width
    )
    first_im = -jnp.dot(sin_one[:, :half_size], shaped, precision=HIGH).reshape(
        outer_size, radix_size, block_width
    )
    second_re = first_re * twist_cos + first_im * twist_sin
    second_im = first_im * twist_cos - first_re * twist_sin
    spec_re = jnp.einsum("amc,mb->abc", second_re, cos_two, precision=HIGH) + jnp.einsum(
        "amc,mb->abc", second_im, sin_two, precision=HIGH
    )
    spec_im = jnp.einsum("amc,mb->abc", second_im, cos_two, precision=HIGH) - jnp.einsum(
        "amc,mb->abc", second_re, sin_two, precision=HIGH
    )
    return (spec_re, spec_im)


def inverse_dft(spec_re, spec_im, tables, radix_size):
    cos_one, sin_one, twist_cos, twist_sin, cos_two, sin_two = tables
    outer_size = cos_one.shape[0]
    half_size = outer_size // 2
    block_width = spec_re.shape[2]
    back_re = jnp.einsum("abc,mb->amc", spec_re, cos_two, precision=HIGH) - jnp.einsum(
        "abc,mb->amc", spec_im, sin_two, precision=HIGH
    )
    back_im = jnp.einsum("abc,mb->amc", spec_re, sin_two, precision=HIGH) + jnp.einsum(
        "abc,mb->amc", spec_im, cos_two, precision=HIGH
    )
    turned_re = (back_re * twist_cos - back_im * twist_sin).reshape(
        outer_size, radix_size * block_width
    )
    turned_im = (back_re * twist_sin + back_im * twist_cos).reshape(
        outer_size, radix_size * block_width
    )
    result = jnp.dot(cos_one[:half_size], turned_re, precision=HIGH) - jnp.dot(
        sin_one[:half_size], turned_im, precision=HIGH
    )
    return result.reshape(half_size * radix_size, block_width) / (outer_size * radix_size)


def long_convolve(gated_slab, filter_slab):
    length, channels = gated_slab.shape
    block_width = min(128, channels)
    tables = dft_tables(length, RADIX)

    def one_block(block_index, output):
        offset = block_index * block_width
        signal = lax.dynamic_slice_in_dim(gated_slab, offset, block_width, 1).astype(jnp.float32)
        kernel_block = lax.dynamic_slice_in_dim(filter_slab, offset, block_width, 1).astype(
            jnp.float32
        )
        sig_re, sig_im = forward_dft(signal, tables, RADIX)
        ker_re, ker_im = forward_dft(kernel_block, tables, RADIX)
        prod_re = sig_re * ker_re - sig_im * ker_im
        prod_im = sig_re * ker_im + sig_im * ker_re
        result = inverse_dft(prod_re, prod_im, tables, RADIX)
        return lax.dynamic_update_slice_in_dim(output, result, offset, 1)

    return lax.fori_loop(
        0, channels // block_width, one_block, jnp.zeros((length, channels), jnp.float32)
    )


def make_response(gated_slab, filter_slab, skip_gain):
    long_part = long_convolve(gated_slab, filter_slab)
    return (long_part + skip_gain * gated_slab.astype(jnp.float32)).astype(jnp.bfloat16)


def combine_rows(query_part, response_part):
    return (query_part.astype(jnp.float32) * response_part.astype(jnp.float32)).astype(jnp.bfloat16)


def on_device(projected, short_taps, long_filter, skip_gain):
    kernel_size = short_taps.shape[0]
    tok_rows = projected[0]
    filter_slab = lax.all_gather(long_filter, "dp", axis=0, tiled=True)
    stream_slab = lax.all_to_all(tok_rows, "ctx", split_axis=2, concat_axis=0, tiled=True)
    extended = jnp.pad(stream_slab, ((kernel_size - 1, 0), (0, 0), (0, 0)))
    query_slab, gated_slab = causal_short(extended, short_taps, kernel_size)
    response_slab = make_response(gated_slab, filter_slab, skip_gain)
    mixed = lax.all_to_all(
        combine_rows(query_slab, response_slab), "ctx", split_axis=0, concat_axis=1, tiled=True
    )
    return mixed[None]


def solution(mesh):
    return jax.shard_map(
        on_device,
        mesh=mesh,
        in_specs=(P("dp", "ctx", None, None), P(None, None, "ctx"), P("dp", "ctx"), P("ctx")),
        out_specs=P("dp", "ctx", None),
        check_vma=False,
    )
```

profile of v0, /device:TPU:0, one launch (start us, length us, event | category | flops | bytes accessed | tf_op | source)
XLA Modules:
  0.0 225.1 jit_solution(1443863807638157853)
XLA Ops:
  6.5 7.2 %copy.33 = bf16[1,128,3,4096]{1,2,3,0:T(4,128)(2,1)} copy(bf16[1,128,3,4096]{3,1,2,0:T(8,128)(2,1)} %param.6) | data formatting | bytes 6291456 | tf_op args[0]
  13.8 5.0 %all-to-all-start = ((bf16[128,3,4096]{0,1,2:T(4,128)(2,1)}), bf16[128,3,4096]{0,1,2:T(4,128)(2,1)}, u32[]{:S(2)}, u32[]{:S(2)}) async-start(bf16[128,3,4096]{0,1,2:T(4,128)(2,1)} %bitcast.224), calls=%async_computation | async-start | bytes 8388608 | tf_op jit(solution)/shard_map/all_to_all | solution.py:138
  19.6 48.0 %all-to-all-done = bf16[128,3,4096]{0,1,2:T(4,128)(2,1)} async-done(((bf16[128,3,4096]{0,1,2:T(4,128)(2,1)}), bf16[128,3,4096]{0,1,2:T(4,128)(2,1)}, u32[]{:S(2)}, u32[]{:S(2)}) %all-to-all-start) | async-done | bytes 3145760 | tf_op jit(solution)/shard_map/all_to_all | solution.py:138
  67.6 5.5 %copy.34 = bf16[4,128,3,1024]{3,1,0,2:T(8,128)(2,1)S(1)} copy(bf16[4,128,3,1024]{1,2,3,0:T(4,128)(2,1)} %bitcast.3) | data formatting | bytes 6291456 | tf_op jit(solution)/shard_map/all_to_all | solution.py:138
  73.1 0.9 pad_convert_fusion
  74.0 1.9 fusion.123
  75.9 2.6 %copy-done = f32[512,3,1024]{2,0,1:T(8,128)} copy-done((f32[512,3,1024]{2,0,1:T(8,128)}, f32[512,3,1024]{2,0,1:T(8,128)S(1)}, u32[]{:S(2)}) %copy-start) | copy-done | bytes 6291480
  78.6 1.3 fusion.128
  80.1 115.5 %while.15 = (s32[]{:T(128)}, f32[512,1024]{1,0:T(8,128)S(1)}, bf16[512,1024]{1,0:T(8,128)(2,1)}, f32[16,16]{1,0:T(8,128)S(1)}, f32[16,16]{1,0:T(8,128)S(1)}, /*i...) while((s32[]{:T(128)}, f32[512,1024]{1,0:T(8,128)S(1)}, ...), condition=%wide.region_1.2_spmd.clone.clone, body=%wide.region_0.1_spmd.clone.clone.sunk | while | flops 1288484864 | bytes 33853592 | solution.py:120
  80.3 1.0 constant_dynamic-slice_fusion.3
  84.6 0.8 convolution_subtract_fusion.6
  89.2 0.9 multiply_add_fusion.4
  92.3 0.9 multiply_add_fusion.5
  94.7 1.0 constant_dynamic-slice_fusion.3
  99.0 0.8 convolution_subtract_fusion.6
  102.1 0.8 convolution_add_fusion.5
  103.6 0.9 multiply_add_fusion.4
  106.7 0.9 multiply_add_fusion.5
  109.1 1.0 constant_dynamic-slice_fusion.3
  113.4 0.8 convolution_subtract_fusion.6
  116.5 0.8 convolution_add_fusion.5
  118.0 0.9 multiply_add_fusion.4
  121.1 0.9 multiply_add_fusion.5
  123.5 1.0 constant_dynamic-slice_fusion.3
  127.8 0.8 convolution_subtract_fusion.6
  130.9 0.8 convolution_add_fusion.5
  132.4 0.9 multiply_add_fusion.4
  135.5 0.9 multiply_add_fusion.5
  138.0 1.0 constant_dynamic-slice_fusion.3
  142.2 0.8 convolution_subtract_fusion.6
  145.3 0.8 convolution_add_fusion.5
  146.8 0.9 multiply_add_fusion.4
  149.9 0.9 multiply_add_fusion.5
  152.4 1.0 constant_dynamic-slice_fusion.3
  156.6 0.8 convolution_subtract_fusion.6
  161.2 0.9 multiply_add_fusion.4
  164.4 0.9 multiply_add_fusion.5
  166.8 1.0 constant_dynamic-slice_fusion.3
  171.1 0.8 convolution_subtract_fusion.6
  175.6 0.9 multiply_add_fusion.4
  178.8 0.9 multiply_add_fusion.5
  181.2 1.0 constant_dynamic-slice_fusion.3
  185.5 0.8 convolution_subtract_fusion.6
  190.0 0.9 multiply_add_fusion.4
  193.2 0.9 multiply_add_fusion.5
  195.6 3.8 %fusion.126 = bf16[512,1024]{1,0:T(8,128)(2,1)S(1)} fusion(f32[512,1024]{1,0:T(8,128)S(1)} %get-tuple-element.246, f32[512,3,1024]{2,0,1:T(8,128)} %copy-done, f32[1024]{0:T(1024)S(1)} %copy-done.2), kind=kLoop, calls=%fused_computation.151 | loop fusion | flops 5242880 | bytes 8392704 | tf_op jit(solution)/shard_map/convert_element_type | solution.py:131
  199.4 16.9 %all_to_all.34 = bf16[4,128,1024]{2,1,0:T(8,128)(2,1)S(1)} all-to-all(bf16[4,128,1024]{2,1,0:T(8,128)(2,1)S(1)} %bitcast.227), channel_id=1, replica_groups=mesh['dp'=8,'ctx'=4] {'ctx'}, dimensions={0} | all-to-all | bytes 2097152 | tf_op jit(solution)/shard_map/all_to_all | solution.py:142
  217.0 1.3 copy.36
  (208 shorter events, 83.7 us)
Async XLA Ops:
  13.8 5.8 %copy-start.1 = (f32[3,3,1024]{2,1,0:T(4,128)S(1)}, f32[3,3,1024]{2,1,0:T(4,128)}, u32[]{:S(2)}) copy-start(f32[3,3,1024]{2,1,0:T(4,128)} %param.7) | copy-start | bytes 110596
  13.8 53.8 %all-to-all-start = ((bf16[128,3,4096]{0,1,2:T(4,128)(2,1)}), bf16[128,3,4096]{0,1,2:T(4,128)(2,1)}, u32[]{:S(2)}, u32[]{:S(2)}) async-start(bf16[128,3,4096]{0,1,2:T(4,128)(2,1)} %bitcast.224), calls=%async_computation | async-start | bytes 8388608 | tf_op jit(solution)/shard_map/all_to_all | solution.py:138
  18.7 61.1 %all-gather.2.cloned.1.call-start = ((), (), s32[]{:S(2)}) async-start(), calls=%async_computation.2 | async-start | bytes 1179648 | tf_op jit(solution)/shard_map/all_gather | solution.py:137
  75.9 2.7 %copy-start = (f32[512,3,1024]{2,0,1:T(8,128)}, f32[512,3,1024]{2,0,1:T(8,128)S(1)}, u32[]{:S(2)}) copy-start(f32[512,3,1024]{2,0,1:T(8,128)S(1)} %fusion.123) | copy-start | bytes 18874372
  80.1 115.5 %copy-start.2 = (f32[1024]{0:T(1024)S(1)}, f32[1024]{0:T(1024)}, u32[]{:S(2)}) copy-start(f32[1024]{0:T(1024)} %param.9) | copy-start | bytes 12292
Sparse Core Ops, SparseCore 0:
  21.7 43.2 all-gather.1
where the time goes:
time: 226 us; the launch traced here: 225 us
  matrix products  96.6 us (43%)
  waiting for transfers between devices  48.7 us (22%)
  local copies, waits for them, and re-layouts  30.4 us (13%)
  blocking collectives  16.9 us (7%)
  between operations  13.5 us (6%)
  other arithmetic  11.9 us (5%)
  starting transfers between devices  5.02 us (2%)
    all_to_all x1, waiting for transfers between devices, on_device(): lax.all_to_all(tok_rows, 'ctx', split_axis=2, concat_axis=0, tiled=True)  48 us
    all_to_all x1, blocking collectives, on_device(): lax.all_to_all(combine_rows(query_slab, response_slab), 'ctx', split_axis...  16.9 us
    dot_general x16, matrix products, forward_dft(): jnp.einsum('amc,mb->abc', second_re, sin_two, precision=HIGH)  13.3 us
    dot_general x16, matrix products, forward_dft(): jnp.einsum('amc,mb->abc', second_im, sin_two, precision=HIGH)  12.1 us
    dot_general x16, matrix products, forward_dft(): jnp.einsum('amc,mb->abc', second_re, cos_two, precision=HIGH)  12 us
    dot_general x16, matrix products, forward_dft(): jnp.einsum('amc,mb->abc', second_im, cos_two, precision=HIGH)  12 us
    unnamed x7, local copies, waits for them, and re-layouts  9.88 us
    dynamic_slice x8, local copies, waits for them, and re-layouts, one_block(): lax.dynamic_slice_in_dim(filter_slab, offset, block_width, 1)  7.97 us
  transfers between devices with their start and end apart: 2, of which 1 were waited for; matrix products, arithmetic and copies ran while one was open for 4% of the time, Pallas kernels for 0%

commit v1 on v0

--- a/solution.py
+++ b/solution.py
@@ -6,6 +6,17 @@
 
 RADIX = 64
 HIGH = lax.Precision.HIGHEST
+
+
+def split_up(array, dim, devices):
+    before, after = (array.shape[:dim], array.shape[dim + 1 :])
+    return jnp.moveaxis(array.reshape(*before, devices, -1, *after), dim, 0)
+
+
+def in_order(parts, dim):
+    lengths = list(parts.shape[1:])
+    lengths[dim] *= parts.shape[0]
+    return jnp.moveaxis(parts, 0, dim).reshape(lengths)
 
 
 def causal_short(extended, taps, kernel_size):
@@ -135,7 +146,15 @@
     kernel_size = short_taps.shape[0]
     tok_rows = projected[0]
     filter_slab = lax.all_gather(long_filter, "dp", axis=0, tiled=True)
-    stream_slab = lax.all_to_all(tok_rows, "ctx", split_axis=2, concat_axis=0, tiled=True)
+    devices, index = (lax.axis_size("ctx"), lax.axis_index("ctx"))
+    blocks = split_up(tok_rows, 2, devices)
+    out = blocks
+    for lap in range(1, devices):
+        target, source = ((index + lap) % devices, (index - lap) % devices)
+        sent = lax.dynamic_index_in_dim(blocks, target, 0)
+        received = lax.ppermute(sent, "ctx", [(i, (i + lap) % devices) for i in range(devices)])
+        out = lax.dynamic_update_slice_in_dim(out, received, source, axis=0)
+    stream_slab = in_order(out, 0)
     extended = jnp.pad(stream_slab, ((kernel_size - 1, 0), (0, 0), (0, 0)))
     query_slab, gated_slab = causal_short(extended, short_taps, kernel_size)
     response_slab = make_response(gated_slab, filter_slab, skip_gain)

time: 226 us -> 210 us (0.929)
  waiting for transfers between devices: 48.7 us -> 30.4 us
    all_to_all x1 -> x0, waiting for transfers between devices: 48 us -> none  [on_device(): lax.all_to_all(tok_rows, 'ctx', split_axis=2, concat_axis=0, tiled=True)]
    ppermute x0 -> x3, waiting for transfers between devices: none -> 30.4 us  [on_device(): lax.ppermute(sent, 'ctx', [(i, (i + lap) % devices) for i in range(device...]
    dynamic_update_slice x0 -> x4, local copies, waits for them, and re-layouts: none -> 6.5 us  [on_device(): out = lax.dynamic_update_slice_in_dim(out, received, source, axis=0)]
    all_to_all x1 -> x0, local copies, waits for them, and re-layouts: 5.51 us -> none  [on_device(): lax.all_to_all(tok_rows, 'ctx', split_axis=2, concat_axis=0, tiled=True)]
    all_to_all x1 -> x0, starting transfers between devices: 4.98 us -> none  [on_device(): lax.all_to_all(tok_rows, 'ctx', split_axis=2, concat_axis=0, tiled=True)]
    ppermute x0 -> x3, starting transfers between devices: none -> 4.4 us  [on_device(): lax.ppermute(sent, 'ctx', [(i, (i + lap) % devices) for i in range(device...]
    unnamed x7, local copies, waits for them, and re-layouts: 9.88 us -> 6.14 us
  transfers between devices with their start and end apart: 2 -> 4, of which waited for: 1 -> 3; matrix products, arithmetic and copies ran while one was open for 4% -> 6% of each run, Pallas kernels for 0% -> 0%
where the time goes in v1:
time: 210 us; the launch traced here: 209 us
  matrix products  96.6 us (46%)
  waiting for transfers between devices  30.4 us (14%)
  local copies, waits for them, and re-layouts  29.6 us (14%)
  blocking collectives  18.4 us (9%)
  other arithmetic  13.9 us (7%)
  between operations  13.6 us (6%)
  starting transfers between devices  4.41 us (2%)
  loops' own time  2.28 us (1%)
    ppermute x3, waiting for transfers between devices, on_device(): lax.ppermute(sent, 'ctx', [(i, (i + lap) % devices) for i in range(device...  30.4 us
    all_to_all x1, blocking collectives, on_device(): lax.all_to_all(combine_rows(query_slab, response_slab), 'ctx', split_axis...  18.4 us
    dot_general x16, matrix products, forward_dft(): jnp.einsum('amc,mb->abc', second_re, sin_two, precision=HIGH)  13.3 us
    dot_general x16, matrix products, forward_dft(): jnp.einsum('amc,mb->abc', second_im, sin_two, precision=HIGH)  12.1 us
    dot_general x16, matrix products, forward_dft(): jnp.einsum('amc,mb->abc', second_re, cos_two, precision=HIGH)  12 us
    dot_general x16, matrix products, forward_dft(): jnp.einsum('amc,mb->abc', second_im, cos_two, precision=HIGH)  12 us
    dynamic_slice x8, local copies, waits for them, and re-layouts, one_block(): lax.dynamic_slice_in_dim(filter_slab, offset, block_width, 1)  7.97 us
    dot_general x8, matrix products, inverse_dft(): jnp.einsum('abc,mb->amc', spec_im, cos_two, precision=HIGH)  7.16 us
  transfers between devices with their start and end apart: 4, of which 3 were waited for; matrix products, arithmetic and copies ran while one was open for 6% of the time, Pallas kernels for 0%

profile of v1, /device:TPU:0, one launch (start us, length us, event | category | flops | bytes accessed | tf_op | source)
XLA Modules:
  0.0 209.2 jit_solution(10733066446679257167)
XLA Ops:
  6.5 3.5 %copy.51 = bf16[1,128,3,4096]{1,3,2,0:T(8,128)(2,1)S(1)} copy(bf16[1,128,3,4096]{3,1,2,0:T(8,128)(2,1)} %param.6) | data formatting | bytes 6291456 | tf_op args[0]
  10.0 1.5 dynamic-slice_bitcast_fusion
  12.0 2.5 %collective-permute-start.1 = (bf16[1,128,3,1024]{1,3,0,2:T(8,128)(2,1)}, bf16[1,128,3,1024]{1,3,0,2:T(8,128)(2,1)}, u32[]{:S(2)}, u32[]{:S(2)}) collective-permute-start(bf16[1,128,3,1024]{1,3,0,2:T(8,128)(2,1)} %get-tuple-element.348), channel_id=1, source_target_pairs={{0,2},{1,3},{2,0},{3,1},{4,6},{5,7},{6,4},{7,5},{8,10},{9,11},{10,... | collective-permute-start | bytes 2359304 | tf_op jit(solution)/shard_map/ppermute | solution.py:155
  14.5 1.4 collective-permute-start.2
  16.1 15.4 %collective-permute-done = bf16[1,128,3,1024]{1,3,0,2:T(8,128)(2,1)} collective-permute-done((bf16[1,128,3,1024]{1,3,0,2:T(8,128)(2,1)}, bf16[1,128,3,1024]{1,3,0,2:T(8,128)(2,1)}, u32[]{:S(2)}, u32[]{:S(2)}) %collective-permute-start) | collective-permute-done | bytes 786464 | tf_op jit(solution)/shard_map/ppermute | solution.py:155
  31.5 1.2 constant_dynamic-update-slice_fusion.3
  33.2 1.2 constant_dynamic-update-slice_fusion.2
  34.4 14.6 %collective-permute-done.2 = bf16[1,128,3,1024]{1,3,0,2:T(8,128)(2,1)} collective-permute-done((bf16[1,128,3,1024]{1,3,0,2:T(8,128)(2,1)}, bf16[1,128,3,1024]{1,3,0,2:T(8,128)(2,1)}, u32[]{:S(2)}, u32[]{:S(2)}) %collective-permute-start.2) | collective-permute-done | bytes 786464 | tf_op jit(solution)/shard_map/ppermute | solution.py:155
  49.0 1.2 constant_dynamic-update-slice_fusion.1
  50.2 2.8 %copy.58 = bf16[4,128,3,1024]{3,1,0,2:T(8,128)(2,1)} copy(bf16[4,128,3,1024]{1,3,0,2:T(8,128)(2,1)S(1)} %constant_dynamic-update-slice_fusion.1) | data formatting | bytes 6291456 | tf_op jit(solution)/shard_map/dynamic_update_slice | solution.py:156
  53.0 2.8 %pad_convert_fusion = f32[514,3,1024]{2,0,1:T(8,128)S(1)} fusion(bf16[512,3,1024]{2,0,1:T(8,128)(2,1)} %bitcast.235), kind=kLoop, calls=%fused_computation.146 | loop fusion | flops 1579008 | bytes 9461760 | tf_op jit(solution)/shard_map/convert_element_type | solution.py:24
  55.8 1.9 fusion.123
  57.7 2.7 %copy-done = f32[512,3,1024]{2,0,1:T(8,128)} copy-done((f32[512,3,1024]{2,0,1:T(8,128)}, f32[512,3,1024]{2,0,1:T(8,128)S(1)}, u32[]{:S(2)}) %copy-start) | copy-done | bytes 6291480
  60.4 1.3 fusion.128
  61.9 115.7 %while.15 = (s32[]{:T(128)}, f32[512,1024]{1,0:T(8,128)S(1)}, bf16[512,1024]{1,0:T(8,128)(2,1)}, f32[16,16]{1,0:T(8,128)S(1)}, f32[16,16]{1,0:T(8,128)S(1)}, /*i...) while((s32[]{:T(128)}, f32[512,1024]{1,0:T(8,128)S(1)}, ...), condition=%wide.region_1.2_spmd.clone.clone, body=%wide.region_0.1_spmd.clone.clone.sunk | while | flops 1288484864 | bytes 33853592 | solution.py:131
  62.1 1.0 constant_dynamic-slice_fusion.3
  66.4 0.8 convolution_subtract_fusion.6
  71.0 0.9 multiply_add_fusion.4
  74.1 0.9 multiply_add_fusion.5
  76.6 1.0 constant_dynamic-slice_fusion.3
  80.8 0.8 convolution_subtract_fusion.6
  85.4 0.9 multiply_add_fusion.4
  88.6 0.9 multiply_add_fusion.5
  91.0 1.0 constant_dynamic-slice_fusion.3
  95.3 0.8 convolution_subtract_fusion.6
  99.8 0.9 multiply_add_fusion.4
  103.0 0.9 multiply_add_fusion.5
  105.4 1.0 constant_dynamic-slice_fusion.3
  114.3 0.9 multiply_add_fusion.4
  117.4 0.9 multiply_add_fusion.5
  119.8 1.0 constant_dynamic-slice_fusion.3
  128.7 0.9 multiply_add_fusion.4
  131.8 0.9 multiply_add_fusion.5
  134.2 1.0 constant_dynamic-slice_fusion.3
  138.5 0.8 convolution_subtract_fusion.6
  143.1 0.9 multiply_add_fusion.4
  146.2 0.9 multiply_add_fusion.5
  148.6 1.0 constant_dynamic-slice_fusion.3
  152.9 0.8 convolution_subtract_fusion.6
  157.5 0.9 multiply_add_fusion.4
  160.6 0.9 multiply_add_fusion.5
  163.1 1.0 constant_dynamic-slice_fusion.3
  171.9 0.9 multiply_add_fusion.4
  175.1 0.9 multiply_add_fusion.5
  177.7 3.8 %fusion.126 = bf16[512,1024]{1,0:T(8,128)(2,1)S(1)} fusion(f32[512,1024]{1,0:T(8,128)S(1)} %get-tuple-element.246, f32[512,3,1024]{2,0,1:T(8,128)} %copy-done, f32[1024]{0:T(1024)S(1)} %copy-done.2), kind=kLoop, calls=%fused_computation.151 | loop fusion | flops 5242880 | bytes 8392704 | tf_op jit(solution)/shard_map/convert_element_type | solution.py:142
  181.5 18.4 %all_to_all.16 = bf16[4,128,1024]{2,1,0:T(8,128)(2,1)S(1)} all-to-all(bf16[4,128,1024]{2,1,0:T(8,128)(2,1)S(1)} %bitcast.237), channel_id=1, replica_groups=mesh['dp'=8,'ctx'=4] {'ctx'}, dimensions={0} | all-to-all | bytes 2097152 | tf_op jit(solution)/shard_map/all_to_all | solution.py:161
  200.0 0.8 copy.59
  200.8 1.6 broadcast_in_dim.5
  (216 shorter events, 88.6 us)
Async XLA Ops:
  6.5 55.1 %all-gather.2.cloned.1.call-start = ((), (), s32[]{:S(2)}) async-start(), calls=%async_computation.1 | async-start | bytes 1179648 | tf_op jit(solution)/shard_map/all_gather | solution.py:148
  10.0 6.1 %copy-start.1 = (f32[3,3,1024]{2,1,0:T(4,128)S(1)}, f32[3,3,1024]{2,1,0:T(4,128)}, u32[]{:S(2)}) copy-start(f32[3,3,1024]{2,1,0:T(4,128)} %param.7) | copy-start | bytes 110596
  11.5 20.0 %collective-permute-start = (bf16[1,128,3,1024]{1,3,0,2:T(8,128)(2,1)}, bf16[1,128,3,1024]{1,3,0,2:T(8,128)(2,1)}, u32[]{:S(2)}, u32[]{:S(2)}) collective-permute-start(bf16[1,128,3,1024]{1,3,0,2:T(8,128)(2,1)} %get-tuple-element.349), channel_id=1, source_target_pairs={{0,1},{1,2},{2,3},{3,0},{4,5},{5,6},{6,7},{7,4},{8,9},{9,10},{10,1... | collective-permute-start | bytes 2359304 | tf_op jit(solution)/shard_map/ppermute | solution.py:155
  12.0 21.2 %collective-permute-start.1 = (bf16[1,128,3,1024]{1,3,0,2:T(8,128)(2,1)}, bf16[1,128,3,1024]{1,3,0,2:T(8,128)(2,1)}, u32[]{:S(2)}, u32[]{:S(2)}) collective-permute-start(bf16[1,128,3,1024]{1,3,0,2:T(8,128)(2,1)} %get-tuple-element.348), channel_id=1, source_target_pairs={{0,2},{1,3},{2,0},{3,1},{4,6},{5,7},{6,4},{7,5},{8,10},{9,11},{10,... | collective-permute-start | bytes 2359304 | tf_op jit(solution)/shard_map/ppermute | solution.py:155
  14.5 34.5 %collective-permute-start.2 = (bf16[1,128,3,1024]{1,3,0,2:T(8,128)(2,1)}, bf16[1,128,3,1024]{1,3,0,2:T(8,128)(2,1)}, u32[]{:S(2)}, u32[]{:S(2)}) collective-permute-start(bf16[1,128,3,1024]{1,3,0,2:T(8,128)(2,1)} %get-tuple-element.347), channel_id=1, source_target_pairs={{0,3},{1,0},{2,1},{3,2},{4,7},{5,4},{6,5},{7,6},{8,11},{9,8},{10,9... | collective-permute-start | bytes 2359304 | tf_op jit(solution)/shard_map/ppermute | solution.py:155
  57.7 2.7 %copy-start = (f32[512,3,1024]{2,0,1:T(8,128)}, f32[512,3,1024]{2,0,1:T(8,128)S(1)}, u32[]{:S(2)}) copy-start(f32[512,3,1024]{2,0,1:T(8,128)S(1)} %fusion.123) | copy-start | bytes 18874372
  61.9 115.8 %copy-start.2 = (f32[1024]{0:T(1024)S(1)}, f32[1024]{0:T(1024)}, u32[]{:S(2)}) copy-start(f32[1024]{0:T(1024)} %param.9) | copy-start | bytes 12292
Sparse Core Ops, SparseCore 0:
  16.1 40.3 all-gather.1
